TPU v7x, 32 devices: a whole 2x2x4 slice. The times are simulated.
32 devices in a mesh: gx: 4 (over y, x), gy: 2 (over core), gz: 4 (over z).
Axes of the slice: x: 2, y: 2, z: 4, core: 2. Of those that a mesh axis runs over, the one named last changes fastest.
Arguments:
- offsets: float32 [3, 8, 4, 8, 128], P(None, 'gx', 'gy', 'gz'), may hold values from 0 to 1
- velocity: float32 [3, 8, 4, 8, 128], P(None, 'gx', 'gy', 'gz'), may hold values from -3 to 3
- density: float32 [8, 4, 8, 128], P('gx', 'gy', 'gz'), may hold values from 0.98 to 1.02
- mass: float32 [8, 4, 8, 128], P('gx', 'gy', 'gz'), may hold values from 0.008 to 0.024
- occupancy: int32 [8, 4, 8], P('gx', 'gy', 'gz'), may hold values from 32 to 128, as said below
- move_direction: int32 [8, 4, 8, 128], P('gx', 'gy', 'gz'), may hold values from 0 to 2, as said below
- move_slot: int32 [8, 4, 8, 128], P('gx', 'gy', 'gz'), may hold values from 0 to 127, as said below
Outputs:
- position_next: float32 [3, 8, 4, 8, 128], P(None, 'gx', 'gy', 'gz')
- velocity_next: float32 [3, 8, 4, 8, 128], P(None, 'gx', 'gy', 'gz')
- density_next: float32 [8, 4, 8, 128], P('gx', 'gy', 'gz')
- arrivals: float32 [7, 2, 4, 2, 4, 128], P(None, None, 'gx', 'gy', 'gz')
Inputs may be any that keep to these rules, and one draw needn't show every extreme that they name: Slots 0 to occupancy - 1 of a cell are live; some cell has all 128 slots live. `move_direction`: 0 on every slot that is not live. `move_slot`: among the live particles of one device with the same nonzero move_direction the slots are distinct, so at most 128 leave a device in one direction; some device sends exactly 128 in one direction. 0 where move_direction is 0.
All inputs are finite; a program needn't handle non-finite values.
Results may differ from a plain program's by a relative error of at most 0.0003.
Values sent between devices are 32-bit elements; how exact they have to be, the bound alone decides.
No kernel may reach another device: no remote copies, remote signals or barrier semaphores. Data moves between devices by JAX's collectives and lax.ppermute only.
A program may use at most 64 MiB of HBM per device.

v0:
```python
import functools
import math

import jax
import jax.numpy as jnp
from jax import lax
from jax.experimental import pallas as pl
from jax.experimental.pallas import tpu as pltpu
from jax.sharding import PartitionSpec as P


MOVES = 128

SMOOTH = 0.5
KERNEL_NORM = 21.0 / (16.0 * math.pi * SMOOTH**3)
GRADIENT = 5.0 * KERNEL_NORM / SMOOTH**2
SOUND_SPEED = 10.0
STIFFNESS = SOUND_SPEED**2 / 7.0
VISCOSITY = 0.1
GRAVITY = 1.0
TIME_STEP = 0.1
HALF_STEP = 0.05

FIELDS = 8
TINY = 1e-24
VISC_SCALE = 2.0 * VISCOSITY * SOUND_SPEED * SMOOTH
SOFTENING = 0.01 * SMOOTH * SMOOTH
REACH = 2.0 * SMOOTH


def exchange(tiles, axis, dim):
    count, length = lax.axis_size(axis), tiles.shape[dim]
    last = lax.slice_in_dim(tiles, length - 1, length, axis=dim)
    first = lax.slice_in_dim(tiles, 0, 1, axis=dim)
    at = lax.axis_index(axis)
    if count == 1:
        before = after = jnp.zeros_like(first)
    elif count == 2:
        got = lax.ppermute(jnp.where(at == 0, last, first), axis, [(0, 1), (1, 0)])
        before = jnp.where(at == 0, 0.0, got)
        after = jnp.where(at == 0, got, 0.0)
    else:
        before = lax.ppermute(last, axis, [(i, (i + 1) % count) for i in range(count)])
        after = lax.ppermute(first, axis, [(i, (i - 1) % count) for i in range(count)])
        before = jnp.where(at == 0, 0.0, before)
        after = jnp.where(at == count - 1, 0.0, after)
    return jnp.concatenate([before, tiles, after], axis=dim)


def with_halo(tiles):
    for axis, dim in (("gy", 1), ("gz", 2), ("gx", 0)):
        tiles = exchange(tiles, axis, dim)
    return tiles


def split3(values):
    high = values.astype(jnp.bfloat16).astype(jnp.float32)
    left = values - high
    middle = left.astype(jnp.bfloat16).astype(jnp.float32)
    return high, middle, left - middle


def split2(values):
    high = values.astype(jnp.bfloat16).astype(jnp.float32)
    return high, (values - high).astype(jnp.bfloat16).astype(jnp.float32)


def squares(tile):
    product = tile * tile
    mixed = tile[0:3] * tile[3:6]
    return product[0:1] + product[1:2] + product[2:3], mixed[0:1] + mixed[1:2] + mixed[2:3]


def near_side(high, middle):
    square, mixed = squares(high + middle)
    extra = jnp.concatenate([square, mixed] + [jnp.zeros_like(square)] * 6, 0)
    row = lax.broadcasted_iota(jnp.int32, extra.shape, 0)
    extra_high, extra_middle, extra_low = split3(extra)
    extra_high = jnp.where((row >= 2) & (row < 5), 1.0, extra_high)
    pieces = [high, middle, high, middle, extra_high, extra_middle, extra_low, jnp.zeros_like(high)]
    return jnp.concatenate(pieces, 0).astype(jnp.bfloat16)


DEPTH = 8 * FIELDS


def own_side(tile):
    high, middle = split2(tile)
    square, mixed = squares(high + middle)
    zero, one = jnp.zeros_like(square), jnp.ones_like(square)
    sides = []
    for order, value, marks in (
        (lambda t: jnp.concatenate([-2.0 * t[0:3]] + [zero] * 5, 0), square, [one, zero]),
        (lambda t: -jnp.concatenate([t[3:6], t[0:3], zero, zero], 0), mixed, [zero, one]),
    ):
        rest = jnp.concatenate(marks + [zero] * 6, 0)
        first = jnp.concatenate(marks + list(split3(value)) + [zero] * 3, 0)
        pieces = [order(high)] * 2 + [order(middle)] * 2 + [first, rest, rest]
        pieces += [jnp.zeros_like(tile)] * (16 - len(pieces))
        sides.append(jnp.transpose(jnp.concatenate(pieces, 0)))
    return jnp.concatenate(sides, 0).astype(jnp.bfloat16)


def pressure_rows(tile):
    rho, mass = tile[6:7], tile[7:8]
    safe = jnp.where(mass > 0, rho, 1.0)
    square = safe * safe
    return safe * (1.0 / VISC_SCALE), STIFFNESS * (square * square * square * safe - 1.0) / square


def count_cells(halo_ref, counts):
    for x in range(halo_ref.shape[0]):
        for y in range(halo_ref.shape[1]):
            live = (halo_ref[x, y, :, 7] > 0).astype(jnp.float32)
            column = jnp.sum(live, axis=1, keepdims=True).astype(jnp.int32)
            for z in range(halo_ref.shape[2]):
                counts[x, y, z] = column[z, 0]


def compact(halo_ref, counts, near, blocks, cells):
    lane = lax.broadcasted_iota(jnp.int32, (FIELDS, 128), 1)
    row = lax.broadcasted_iota(jnp.int32, (FIELDS, 128), 0)
    places = all_cells(cells)
    at = [jnp.int32(0)] * len(places)
    for sx in range(3):
        for sy in range(3):
            for sz in range(3):
                shift = jnp.where(row == 0, sx - 1.5, jnp.where(row == 1, sy - 1.5, jnp.where(row == 2, sz - 1.5, 0.0)))
                for c, (cx, cy, cz) in enumerate(places):
                    block, inside = lax.shift_right_logical(at[c], 7), at[c] & 127
                    rolled = pltpu.roll(halo_ref[cx + sx, cy + sy, cz + sz] + shift, inside, axis=1)
                    pltpu.store(near.at[c, block], rolled, mask=lane >= inside)
                    near[c, block + 1] = rolled
                    at[c] = at[c] + counts[cx + sx, cy + sy, cz + sz]
    for c in range(len(places)):
        block, inside = lax.shift_right_logical(at[c], 7), at[c] & 127
        zeros = jnp.zeros((FIELDS, 128), jnp.float32)
        pltpu.store(near.at[c, block], zeros, mask=lane >= inside)
        near[c, block + 1] = zeros
        blocks[c] = lax.shift_right_logical(at[c] + 255, 8)


def own_kernel(cells, tiles_ref, own_ref, terms_ref):
    row = lax.broadcasted_iota(jnp.int32, (FIELDS, 128), 0)
    for index, place in enumerate(all_cells(cells)):
        tile = tiles_ref[place] - jnp.where(row < 3, 0.5, 0.0)
        own_ref[index] = own_side(tile)
        columns = jnp.transpose(jnp.concatenate(list(pressure_rows(tile)) + [jnp.zeros((6, 128), jnp.float32)], 0))
        for k in range(2):
            terms_ref[index, k] = jnp.broadcast_to(columns[:, k : k + 1], (128, 128))


def pair_sums(counts, near, blocks, own, terms, slots, total, cell, index):
    cx, cy, cz = cell
    total[index] = jnp.zeros(total.shape[1:], jnp.float32)
    here = counts[cx + 1, cy + 1, cz + 1]
    chunks = lax.shift_right_logical(here + 15, 4)
    count = blocks[index]

    def run(rows):
        def products(block, slot):
            pairs, listed = slot
            sides = []
            for side in range(2):
                tile = near[index, 2 * block + side]
                high, middle = split2(tile)
                sides.append(near_side(high, middle))
                listed[side, 0:3] = high[0:3] + middle[0:3]
                for k, value in enumerate((*pressure_rows(tile), GRADIENT * tile[7:8])):
                    listed[side, 3 + k : 4 + k] = value
            right = jnp.concatenate(sides, 1)
            for k in range(2):
                pairs[k, 0:rows] = jnp.dot(own[index, pl.ds(128 * k, rows), 0:DEPTH], right, preferred_element_type=jnp.float32)

        def add(slot):
            pairs, listed = slot
            js = [[jnp.broadcast_to(listed[side, k : k + 1], (8, 128)) for k in range(6)] for side in range(2)]
            for part in range(rows // 8):
                at = pl.ds(8 * part, 8)
                qi, ai = terms[index, 0, at], terms[index, 1, at]
                sums = [total[index, k, at] for k in range(5)]
                for side, (xj, yj, zj, qj, aj, mj) in enumerate(js):
                    lanes = pl.ds(128 * side, 128)
                    dist_sq, along = jnp.maximum(pairs[0, at, lanes], TINY), pairs[1, at, lanes]
                    dist = dist_sq * lax.rsqrt(dist_sq)
                    fall = jnp.maximum(1.0 - (dist if REACH == 1.0 else dist * (1.0 / REACH)), 0.0)
                    weight = fall * fall * fall * mj
                    viscous = jnp.minimum(along, 0.0) / ((dist_sq + SOFTENING) * (qi + qj))
                    push = weight * (ai + aj - viscous)
                    sums[0] += push
                    sums[1] += push * xj
                    sums[2] += push * yj
                    sums[3] += push * zj
                    sums[4] += weight * along
                for k in range(5):
                    total[index, k, at] = sums[k]

        products(0, slots[0])

        def step(pair, carry):
            products(2 * pair + 1, slots[1])
            add(slots[0])
            products(2 * pair + 2, slots[0])
            add(slots[1])
            return carry

        lax.fori_loop(0, lax.shift_right_logical(count, 1), step, 0)
        pl.when((count & 1) == 1)(lambda: add(slots[0]))

    for rows in range(16, 129, 16):
        pl.when(chunks == rows // 16)(functools.partial(run, rows))


def over_cells(halo_ref, own, terms, scratch, cells, visit):
    counts, blocks, near, total = scratch[:4]
    count_cells(halo_ref, counts)
    compact(halo_ref, counts, near, blocks, cells)

    def one(index, carry):
        cz = index % cells[2]
        cy = lax.div(index, cells[2]) % cells[1]
        cx = lax.div(index, cells[1] * cells[2])
        pair_sums(counts, near, blocks, own, terms, (scratch[4:6], scratch[6:8]), total, (cx, cy, cz), index)
        return carry

    lax.fori_loop(0, cells[0] * cells[1] * cells[2], one, 0)
    ones = jnp.ones((16, 128), jnp.bfloat16)
    lane = lax.broadcasted_iota(jnp.int32, (1, 128), 1)
    for index in range(cells[0] * cells[1] * cells[2]):
        cx, cy, cz = index // (cells[1] * cells[2]), index // cells[2] % cells[1], index % cells[2]
        flat = total[index, 1:4].reshape(3 * 128, 128)
        high = flat.astype(jnp.bfloat16)
        middle = (flat - high.astype(jnp.float32)).astype(jnp.bfloat16)
        summed = sum(
            lax.dot_general(ones, piece, (((1,), (1,)), ((), ())), preferred_element_type=jnp.float32)[0:1]
            for piece in (high, middle)
        )
        across = [jnp.sum(jnp.transpose(total[index, k]), axis=0, keepdims=True) for k in (0, 4)]
        sums = [across[0]] + [summed[:, 128 * k : 128 * (k + 1)] for k in range(3)] + [across[1]]
        tile = halo_ref[cx + 1, cy + 1, cz + 1]
        live = lane < counts[cx + 1, cy + 1, cz + 1]
        place = sum(split2(tile[0:3] - 0.5))
        accel = [jnp.where(live, place[k : k + 1] * sums[0] - sums[k + 1], 0.0) for k in range(3)]
        accel[2] = accel[2] - GRAVITY
        visit(cx, cy, cz, accel, jnp.where(live, -sums[4], 0.0))


def scratch_for(halo_shape, cells):
    own = cells[0] * cells[1] * cells[2]
    slot = [pltpu.VMEM((2, 128, 256), jnp.float32), pltpu.VMEM((2, FIELDS, 128), jnp.float32)]
    return [
        pltpu.SMEM(halo_shape[:3], jnp.int32),
        pltpu.SMEM((own,), jnp.int32),
        pltpu.VMEM((own, 32, FIELDS, 128), jnp.float32),
        pltpu.VMEM((own, 5, 128, 128), jnp.float32),
        *slot,
        *slot,
    ]


PREPARE = pl.CostEstimate(flops=10**9, bytes_accessed=10**6, transcendentals=0)


def call(kernel, cells, outs, args, scratch=(), source=pltpu.VMEM, cost=None):
    whole = pl.BlockSpec(memory_space=pltpu.VMEM)
    return pl.pallas_call(
        functools.partial(kernel, cells),
        out_shape=[out if hasattr(out, "dtype") else jax.ShapeDtypeStruct(out, jnp.float32) for out in outs],
        in_specs=[pl.BlockSpec(memory_space=source)] * len(args),
        out_specs=[whole] * len(outs),
        scratch_shapes=list(scratch),
        cost_estimate=cost,
        compiler_params=pltpu.CompilerParams(vmem_limit_bytes=16 * 1024 * 1024),
    )(*args)


def all_cells(cells):
    return [(x, y, z) for x in range(cells[0]) for y in range(cells[1]) for z in range(cells[2])]


def state_kernel(cells, *refs):
    sources, (state_ref, target_ref), copies, arrived = refs[:7], refs[7:9], refs[9:16], refs[16]
    moves = [pltpu.make_async_copy(sources[k], copies[k], arrived.at[k]) for k in range(len(sources))]
    for move in moves:
        move.start()
    for move in moves:
        move.wait()
    offsets_ref, velocity_ref, density_ref, mass_ref, direction_ref, slot_ref, occupancy_ref = copies
    lane = lax.broadcasted_iota(jnp.int32, (1, 128), 1)
    for cx, cy, cz in all_cells(cells):
        here = pl.ds(cz, 1)
        for k in range(3):
            state_ref[cx, cy, cz, k : k + 1] = offsets_ref[k, cx, cy, here]
            state_ref[cx, cy, cz, k + 3 : k + 4] = velocity_ref[k, cx, cy, here]
        state_ref[cx, cy, cz, 6:7] = density_ref[cx, cy, here]
        live = lane < occupancy_ref[cx, cy, cz]
        state_ref[cx, cy, cz, 7:8] = jnp.where(live, mass_ref[cx, cy, here], 0.0)
        way, slot = direction_ref[cx, cy, here], slot_ref[cx, cy, here]
        target = jnp.where(way == 1, slot, jnp.where(way == 2, slot + MOVES, -1))
        target_ref[cx, cy, here] = jnp.where(live, target, -2)


def half_kernel(cells, halo_ref, own_ref, terms_ref, half_ref, *scratch):
    def visit(cx, cy, cz, accel, rate):
        tile = halo_ref[cx + 1, cy + 1, cz + 1]
        change = jnp.concatenate([tile[3:6]] + accel + [rate, jnp.zeros_like(rate)], 0)
        half_ref[cx, cy, cz] = tile + HALF_STEP * change

    over_cells(halo_ref, own_ref, terms_ref, scratch, cells, visit)


def last_kernel(cells, halo_ref, own_ref, terms_ref, state_ref, target_ref, lower_ref, upper_ref, kept_ref, *scratch):
    slots = lax.broadcasted_iota(jnp.int32, (2 * MOVES, 128), 0)
    row = lax.broadcasted_iota(jnp.int32, (FIELDS, 128), 0)
    lists = [jnp.zeros((FIELDS, 2 * MOVES), jnp.float32)]

    def visit(cx, cy, cz, accel, rate):
        tile = state_ref[cx, cy, cz]
        half = halo_ref[cx + 1, cy + 1, cz + 1]
        change = jnp.concatenate([half[3:6]] + accel + [rate, jnp.zeros_like(rate)], 0)
        new = tile + TIME_STEP * change
        target = target_ref[cx, cy, pl.ds(cz, 1)]
        kept_ref[cx, cy, cz] = jnp.where(target == -1, new, 0.0)
        chosen = (slots == target).astype(jnp.float32).astype(jnp.bfloat16)
        place = jnp.where(row == 0, float(cx), jnp.where(row == 1, float(cy), jnp.where(row == 2, float(cz), 0.0)))
        record = jnp.where(row == 7, 1.0, new + place)
        for piece in split3(record):
            lists[0] += lax.dot_general(
                piece.astype(jnp.bfloat16), chosen, (((1,), (1,)), ((), ())), preferred_element_type=jnp.float32
            )

    over_cells(halo_ref, own_ref, terms_ref, scratch, cells, visit)
    for side, (out_ref, moved) in enumerate(((lower_ref, -float(cells[0])), (upper_ref, float(cells[0])))):
        half = lists[0][:, MOVES * side : MOVES * (side + 1)]
        out_ref[...] = half + jnp.where(row == 0, moved, 0.0) * half[7:8]


def output_kernel(cells, kept_ref, position_ref, velocity_ref, density_ref):
    for cx, cy, cz in all_cells(cells):
        here = pl.ds(cz, 1)
        for k in range(3):
            position_ref[k, cx, cy, here] = kept_ref[cx, cy, cz, k : k + 1]
            velocity_ref[k, cx, cy, here] = kept_ref[cx, cy, cz, k + 3 : k + 4]
        density_ref[cx, cy, here] = kept_ref[cx, cy, cz, 6:7]


def body(offsets, velocity, density, mass, occupancy, move_direction, move_slot):
    cells = density.shape[:3]
    tiles = (*cells, FIELDS, 128)
    fields = (offsets, velocity, density, mass, move_direction, move_slot, occupancy)
    places = jax.ShapeDtypeStruct(density.shape, jnp.int32)
    fields = tuple(pltpu.with_memory_space_constraint(field, pltpu.HBM) for field in fields)
    staged = [pltpu.VMEM(field.shape, field.dtype) for field in fields[:-1]]
    staged += [pltpu.SMEM(occupancy.shape, occupancy.dtype), pltpu.SemaphoreType.DMA((len(fields),))]
    state, target = call(state_kernel, cells, [tiles, places], fields, staged, source=pltpu.HBM)
    own = cells[0] * cells[1] * cells[2]
    sides = [jax.ShapeDtypeStruct((own, 256, 128), jnp.bfloat16), (own, 2, 128, 128)]
    halo = with_halo(state)
    prepared = call(own_kernel, cells, sides, (state,), cost=PREPARE)
    scratch = scratch_for(halo.shape, cells)
    (half,) = call(half_kernel, cells, [tiles], (halo, *prepared), scratch)
    halo = with_halo(half)
    prepared = call(own_kernel, cells, sides, (half,), cost=PREPARE)
    arguments = (halo, *prepared, state, target)
    lower, upper, kept = call(last_kernel, cells, [(FIELDS, MOVES), (FIELDS, MOVES), tiles], arguments, scratch)
    shapes = [offsets.shape, velocity.shape, density.shape]
    count, at = lax.axis_size("gx"), lax.axis_index("gx")
    position_next, velocity_next, density_next = call(output_kernel, cells, shapes, (kept,), cost=PREPARE)
    if count > 1:
        lower = lax.ppermute(lower, "gx", [(i, (i + 1) % count) for i in range(count)])
        upper = lax.ppermute(upper, "gx", [(i, (i - 1) % count) for i in range(count)])
    lists = jnp.stack([jnp.where(at == 0, 0.0, lower), jnp.where(at == count - 1, 0.0, upper)], 1)
    arrivals = lists[:7].reshape(7, 2, 1, 1, 1, MOVES)
    return (position_next, velocity_next, density_next, arrivals)


def solution(mesh):
    placed = (
        P(None, "gx", "gy", "gz", None),
        P(None, "gx", "gy", "gz", None),
        P("gx", "gy", "gz", None),
        P("gx", "gy", "gz", None),
        P("gx", "gy", "gz"),
        P("gx", "gy", "gz", None),
        P("gx", "gy", "gz", None),
    )
    return jax.shard_map(
        body,
        mesh=mesh,
        in_specs=placed,
        out_specs=(
            P(None, "gx", "gy", "gz", None),
            P(None, "gx", "gy", "gz", None),
            P("gx", "gy", "gz", None),
            P(None, None, "gx", "gy", "gz", None),
        ),
        check_vma=False,
    )
```

profile of v0, /device:TPU:8, one launch (start us, length us, event | category | flops | bytes accessed | tf_op | source)
XLA Modules:
  0.0 58.6 jit_solution(15857085413494821237)
XLA Ops:
  0.6 0.9 %shard_map.102 = (f32[2,2,2,8,128]{4,3,2,1,0:T(8,128)S(1)}, s32[2,2,2,128]{3,2,1,0:T(2,128)S(1)}) custom-call(f32[3,2,2,2,128]{4,3,2,1,0:T(2,128)} %refs_0_.1, f32[3,2,2,2,128]{4,3,2,1,0:T(2,128)} %refs_1_.1, f32[2,2,2,128]{3,2,1,0:T(2,128)} %refs_2_.1, f32[2,2,2,128]{3,2,1,0:T(2,128)} %refs_3_.1, s32[2,2,2,128]{3,2,1,0:T(2,128)} %refs_4_.1, ...), custom_call_target="tpu_custom_call" | custom-call | tf_op jit(solution)/shard_map/pallas_call | solution.py:266
  1.6 0.1 collective-permute-start
  1.7 1.2 %collective-permute-done = f32[2,1,2,8,128]{4,3,2,1,0:T(8,128)S(1)} collective-permute-done((f32[2,1,2,8,128]{4,3,2,1,0:T(8,128)S(1)}, f32[2,1,2,8,128]{4,3,2,1,0:T(8,128)S(1)}, u32[]{:S(2)}, u32[]{:S(2)}) %collective-permute-start) | collective-permute-done | bytes 16416 | tf_op jit(solution)/shard_map/ppermute | solution.py:39
  2.9 1.6 %collective-permute-start.1 = (f32[2,4,1,8,128]{4,3,2,1,0:T(8,128)S(1)}, f32[2,4,1,8,128]{4,3,2,1,0:T(8,128)S(1)}, u32[]{:S(2)}, u32[]{:S(2)}) collective-permute-start(f32[2,4,1,8,128]{4,3,2,1,0:T(8,128)S(1)} %get-tuple-element.38), channel_id=1, source_target_pairs={{0,1},{1,2},{2,3},{3,0},{4,5},{5,6},{6,7},{7,4},{8,9},{9,10},{10,1... | collective-permute-start | bytes 98312 | tf_op jit(solution)/shard_map/ppermute | solution.py:43
  4.5 0.4 collective-permute-start.2
  4.9 1.9 %collective-permute-done.1 = f32[2,4,1,8,128]{4,3,2,1,0:T(8,128)S(1)} collective-permute-done((f32[2,4,1,8,128]{4,3,2,1,0:T(8,128)S(1)}, f32[2,4,1,8,128]{4,3,2,1,0:T(8,128)S(1)}, u32[]{:S(2)}, u32[]{:S(2)}) %collective-permute-start.1) | collective-permute-done | bytes 32800 | tf_op jit(solution)/shard_map/ppermute | solution.py:43
  6.8 1.6 %collective-permute-done.2 = f32[2,4,1,8,128]{4,3,2,1,0:T(8,128)S(1)} collective-permute-done((f32[2,4,1,8,128]{4,3,2,1,0:T(8,128)S(1)}, f32[2,4,1,8,128]{4,3,2,1,0:T(8,128)S(1)}, u32[]{:S(2)}, u32[]{:S(2)}) %collective-permute-start.2) | collective-permute-done | bytes 32800 | tf_op jit(solution)/shard_map/ppermute | solution.py:44
  8.4 1.5 %collective-permute-start.3 = (f32[1,4,4,8,128]{4,3,2,1,0:T(8,128)S(1)}, f32[1,4,4,8,128]{4,3,2,1,0:T(8,128)S(1)}, u32[]{:S(2)}, u32[]{:S(2)}) collective-permute-start(f32[1,4,4,8,128]{4,3,2,1,0:T(8,128)S(1)} %get-tuple-element.34), channel_id=1, source_target_pairs={{0,8},{8,16},{16,24},{24,0},{1,9},{9,17},{17,25},{25,1},{2,10},{10... | collective-permute-start | bytes 196616 | tf_op jit(solution)/shard_map/ppermute | solution.py:43
  10.0 0.7 %shard_map.103 = (bf16[8,256,128]{2,1,0:T(8,128)(2,1)S(1)}, f32[8,2,128,128]{3,2,1,0:T(8,128)S(1)}) custom-call(f32[2,2,2,8,128]{4,3,2,1,0:T(8,128)S(1)} %get-tuple-element.16.tiles_ref.state_ref), custom_call_target="tpu_custom_call" | custom-call | flops 1000000000 | bytes 1000000 | tf_op jit(solution)/shard_map/pallas_call | solution.py:266
  10.7 1.5 %collective-permute-start.4 = (f32[1,4,4,8,128]{4,3,2,1,0:T(8,128)S(1)}, f32[1,4,4,8,128]{4,3,2,1,0:T(8,128)S(1)}, u32[]{:S(2)}, u32[]{:S(2)}) collective-permute-start(f32[1,4,4,8,128]{4,3,2,1,0:T(8,128)S(1)} %get-tuple-element.35), channel_id=1, source_target_pairs={{0,24},{8,0},{16,8},{24,16},{1,25},{9,1},{17,9},{25,17},{2,26},{10... | collective-permute-start | bytes 196616 | tf_op jit(solution)/shard_map/ppermute | solution.py:44
  12.2 2.0 %collective-permute-done.3 = f32[1,4,4,8,128]{4,3,2,1,0:T(8,128)S(1)} collective-permute-done((f32[1,4,4,8,128]{4,3,2,1,0:T(8,128)S(1)}, f32[1,4,4,8,128]{4,3,2,1,0:T(8,128)S(1)}, u32[]{:S(2)}, u32[]{:S(2)}) %collective-permute-start.3) | collective-permute-done | bytes 65568 | tf_op jit(solution)/shard_map/ppermute | solution.py:43
  14.2 0.8 %collective-permute-done.4 = f32[1,4,4,8,128]{4,3,2,1,0:T(8,128)S(1)} collective-permute-done((f32[1,4,4,8,128]{4,3,2,1,0:T(8,128)S(1)}, f32[1,4,4,8,128]{4,3,2,1,0:T(8,128)S(1)}, u32[]{:S(2)}, u32[]{:S(2)}) %collective-permute-start.4) | collective-permute-done | bytes 65568 | tf_op jit(solution)/shard_map/ppermute | solution.py:44
  15.0 10.5 %shard_map.104.tiles_ref = f32[2,2,2,8,128]{4,3,2,1,0:T(8,128)S(1)} custom-call(f32[4,4,4,8,128]{4,3,2,1,0:T(8,128)S(1)} %pad_maximum_fusion.halo_ref, bf16[8,256,128]{2,1,0:T(8,128)(2,1)S(1)} %get-tuple-element.17.own_ref, f32[8,2,128,128]{3,2,1,0:T(8,128)S(1)} %get-tuple-element.18.terms_ref), custom_call_target="tpu_custom_call" | custom-call | tf_op jit(solution)/shard_map/pallas_call | solution.py:266
  25.5 0.1 collective-permute-start.5
  25.6 1.2 %collective-permute-done.5 = f32[2,1,2,8,128]{4,3,2,1,0:T(8,128)S(1)} collective-permute-done((f32[2,1,2,8,128]{4,3,2,1,0:T(8,128)S(1)}, f32[2,1,2,8,128]{4,3,2,1,0:T(8,128)S(1)}, u32[]{:S(2)}, u32[]{:S(2)}) %collective-permute-start.5) | collective-permute-done | bytes 16416 | tf_op jit(solution)/shard_map/ppermute | solution.py:39
  26.8 0.1 collective-permute-start.6
  26.9 2.0 %collective-permute-start.7 = (f32[2,4,1,8,128]{4,3,2,1,0:T(8,128)S(1)}, f32[2,4,1,8,128]{4,3,2,1,0:T(8,128)S(1)}, u32[]{:S(2)}, u32[]{:S(2)}) collective-permute-start(f32[2,4,1,8,128]{4,3,2,1,0:T(8,128)S(1)} %get-tuple-element.37), channel_id=1, source_target_pairs={{0,3},{1,0},{2,1},{3,2},{4,7},{5,4},{6,5},{7,6},{8,11},{9,8},{10,9... | collective-permute-start | bytes 98312 | tf_op jit(solution)/shard_map/ppermute | solution.py:44
  28.9 1.9 %collective-permute-done.6 = f32[2,4,1,8,128]{4,3,2,1,0:T(8,128)S(1)} collective-permute-done((f32[2,4,1,8,128]{4,3,2,1,0:T(8,128)S(1)}, f32[2,4,1,8,128]{4,3,2,1,0:T(8,128)S(1)}, u32[]{:S(2)}, u32[]{:S(2)}) %collective-permute-start.6) | collective-permute-done | bytes 32800 | tf_op jit(solution)/shard_map/ppermute | solution.py:43
  30.8 0.1 collective-permute-done.7
  30.9 5.1 %collective-permute-start.8 = (f32[1,4,4,8,128]{4,3,2,1,0:T(8,128)S(1)}, f32[1,4,4,8,128]{4,3,2,1,0:T(8,128)S(1)}, u32[]{:S(2)}, u32[]{:S(2)}) collective-permute-start(f32[1,4,4,8,128]{4,3,2,1,0:T(8,128)S(1)} %get-tuple-element.32), channel_id=1, source_target_pairs={{0,8},{8,16},{16,24},{24,0},{1,9},{9,17},{17,25},{25,1},{2,10},{10... | collective-permute-start | bytes 196616 | tf_op jit(solution)/shard_map/ppermute | solution.py:43
  35.9 0.7 %shard_map.105 = (bf16[8,256,128]{2,1,0:T(8,128)(2,1)S(1)}, f32[8,2,128,128]{3,2,1,0:T(8,128)S(1)}) custom-call(f32[2,2,2,8,128]{4,3,2,1,0:T(8,128)S(1)} %shard_map.104.tiles_ref), custom_call_target="tpu_custom_call" | custom-call | flops 1000000000 | bytes 1000000 | tf_op jit(solution)/shard_map/pallas_call | solution.py:266
  36.6 0.1 collective-permute-start.9
  36.7 1.3 %collective-permute-done.8 = f32[1,4,4,8,128]{4,3,2,1,0:T(8,128)S(1)} collective-permute-done((f32[1,4,4,8,128]{4,3,2,1,0:T(8,128)S(1)}, f32[1,4,4,8,128]{4,3,2,1,0:T(8,128)S(1)}, u32[]{:S(2)}, u32[]{:S(2)}) %collective-permute-start.8) | collective-permute-done | bytes 65568 | tf_op jit(solution)/shard_map/ppermute | solution.py:43
  38.0 2.9 %collective-permute-done.9 = f32[1,4,4,8,128]{4,3,2,1,0:T(8,128)S(1)} collective-permute-done((f32[1,4,4,8,128]{4,3,2,1,0:T(8,128)S(1)}, f32[1,4,4,8,128]{4,3,2,1,0:T(8,128)S(1)}, u32[]{:S(2)}, u32[]{:S(2)}) %collective-permute-start.9) | collective-permute-done | bytes 65568 | tf_op jit(solution)/shard_map/ppermute | solution.py:44
  41.0 11.3 %shard_map.106 = (f32[8,128]{1,0:T(8,128)S(1)}, f32[8,128]{1,0:T(8,128)S(1)}, f32[2,2,2,8,128]{4,3,2,1,0:T(8,128)S(1)}) custom-call(f32[4,4,4,8,128]{4,3,2,1,0:T(8,128)S(1)} %pad_maximum_fusion.1.halo_ref, bf16[8,256,128]{2,1,0:T(8,128)(2,1)S(1)} %get-tuple-element.19.own_ref, f32[8,2,128,128]{3,2,1,0:T(8,128)S(1)} %get-tuple-element.20.terms_ref, ...), custom_call_target="tpu_custom_call" | custom-call | tf_op jit(solution)/shard_map/pallas_call | solution.py:266
  52.3 1.4 %collective-permute-start.10 = (f32[8,128]{1,0:T(8,128)S(1)}, f32[8,128]{1,0:T(8,128)S(1)}, u32[]{:S(2)}, u32[]{:S(2)}) collective-permute-start(f32[8,128]{1,0:T(8,128)S(1)} %get-tuple-element.26), channel_id=1, source_target_pairs={{0,8},{8,16},{16,24},{24,0},{1,9},{9,17},{17,25},{25,1},{2,10},{10... | collective-permute-start | bytes 12296 | tf_op jit(solution)/shard_map/ppermute | solution.py:370
  53.8 0.6 %shard_map.107 = (f32[3,2,2,2,128]{4,3,2,1,0:T(2,128)}, f32[3,2,2,2,128]{4,3,2,1,0:T(2,128)}, f32[2,2,2,128]{3,2,1,0:T(2,128)}) custom-call(f32[2,2,2,8,128]{4,3,2,1,0:T(8,128)S(1)} %get-tuple-element.22.kept_ref), custom_call_target="tpu_custom_call" | custom-call | flops 1000000000 | bytes 1000000 | tf_op jit(solution)/shard_map/pallas_call | solution.py:266
  54.4 1.5 %collective-permute-start.11 = (f32[8,128]{1,0:T(8,128)S(1)}, f32[8,128]{1,0:T(8,128)S(1)}, u32[]{:S(2)}, u32[]{:S(2)}) collective-permute-start(f32[8,128]{1,0:T(8,128)S(1)} %get-tuple-element.27), channel_id=1, source_target_pairs={{0,24},{8,0},{16,8},{24,16},{1,25},{9,1},{17,9},{25,17},{2,26},{10... | collective-permute-start | bytes 12296 | tf_op jit(solution)/shard_map/ppermute | solution.py:371
  55.9 1.0 %collective-permute-done.10 = f32[8,128]{1,0:T(8,128)S(1)} collective-permute-done((f32[8,128]{1,0:T(8,128)S(1)}, f32[8,128]{1,0:T(8,128)S(1)}, u32[]{:S(2)}, u32[]{:S(2)}) %collective-permute-start.10) | collective-permute-done | bytes 4128 | tf_op jit(solution)/shard_map/ppermute | solution.py:370
  56.9 1.1 %collective-permute-done.11 = f32[8,128]{1,0:T(8,128)S(1)} collective-permute-done((f32[8,128]{1,0:T(8,128)S(1)}, f32[8,128]{1,0:T(8,128)S(1)}, u32[]{:S(2)}, u32[]{:S(2)}) %collective-permute-start.11) | collective-permute-done | bytes 4128 | tf_op jit(solution)/shard_map/ppermute | solution.py:371
  58.0 0.6 %copy.11 = f32[7,2,1,1,1,128]{5,4,3,2,1,0:T(1,128)} copy(f32[7,2,1,1,1,128]{5,0,1,4,3,2:T(8,128)S(1)} %fusion) | data formatting | bytes 14336
  (25 shorter events, 0.2 us)
Async XLA Ops:
  1.6 1.2 %collective-permute-start = (f32[2,1,2,8,128]{4,3,2,1,0:T(8,128)S(1)}, f32[2,1,2,8,128]{4,3,2,1,0:T(8,128)S(1)}, u32[]{:S(2)}, u32[]{:S(2)}) collective-permute-start(f32[2,1,2,8,128]{4,3,2,1,0:T(8,128)S(1)} %slice_select_fusion.1), channel_id=1, source_target_pairs={{0,4},{4,0},{1,5},{5,1},{2,6},{6,2},{3,7},{7,3},{8,12},{12,8},{9,1... | collective-permute-start | bytes 49160 | tf_op jit(solution)/shard_map/ppermute | solution.py:39
  2.9 4.0 %collective-permute-start.1 = (f32[2,4,1,8,128]{4,3,2,1,0:T(8,128)S(1)}, f32[2,4,1,8,128]{4,3,2,1,0:T(8,128)S(1)}, u32[]{:S(2)}, u32[]{:S(2)}) collective-permute-start(f32[2,4,1,8,128]{4,3,2,1,0:T(8,128)S(1)} %get-tuple-element.38), channel_id=1, source_target_pairs={{0,1},{1,2},{2,3},{3,0},{4,5},{5,6},{6,7},{7,4},{8,9},{9,10},{10,1... | collective-permute-start | bytes 98312 | tf_op jit(solution)/shard_map/ppermute | solution.py:43
  4.5 3.9 %collective-permute-start.2 = (f32[2,4,1,8,128]{4,3,2,1,0:T(8,128)S(1)}, f32[2,4,1,8,128]{4,3,2,1,0:T(8,128)S(1)}, u32[]{:S(2)}, u32[]{:S(2)}) collective-permute-start(f32[2,4,1,8,128]{4,3,2,1,0:T(8,128)S(1)} %get-tuple-element.39), channel_id=1, source_target_pairs={{0,3},{1,0},{2,1},{3,2},{4,7},{5,4},{6,5},{7,6},{8,11},{9,8},{10,9... | collective-permute-start | bytes 98312 | tf_op jit(solution)/shard_map/ppermute | solution.py:44
  8.4 5.7 %collective-permute-start.3 = (f32[1,4,4,8,128]{4,3,2,1,0:T(8,128)S(1)}, f32[1,4,4,8,128]{4,3,2,1,0:T(8,128)S(1)}, u32[]{:S(2)}, u32[]{:S(2)}) collective-permute-start(f32[1,4,4,8,128]{4,3,2,1,0:T(8,128)S(1)} %get-tuple-element.34), channel_id=1, source_target_pairs={{0,8},{8,16},{16,24},{24,0},{1,9},{9,17},{17,25},{25,1},{2,10},{10... | collective-permute-start | bytes 196616 | tf_op jit(solution)/shard_map/ppermute | solution.py:43
  10.7 4.3 %collective-permute-start.4 = (f32[1,4,4,8,128]{4,3,2,1,0:T(8,128)S(1)}, f32[1,4,4,8,128]{4,3,2,1,0:T(8,128)S(1)}, u32[]{:S(2)}, u32[]{:S(2)}) collective-permute-start(f32[1,4,4,8,128]{4,3,2,1,0:T(8,128)S(1)} %get-tuple-element.35), channel_id=1, source_target_pairs={{0,24},{8,0},{16,8},{24,16},{1,25},{9,1},{17,9},{25,17},{2,26},{10... | collective-permute-start | bytes 196616 | tf_op jit(solution)/shard_map/ppermute | solution.py:44
  25.5 1.2 %collective-permute-start.5 = (f32[2,1,2,8,128]{4,3,2,1,0:T(8,128)S(1)}, f32[2,1,2,8,128]{4,3,2,1,0:T(8,128)S(1)}, u32[]{:S(2)}, u32[]{:S(2)}) collective-permute-start(f32[2,1,2,8,128]{4,3,2,1,0:T(8,128)S(1)} %slice_select_fusion), channel_id=1, source_target_pairs={{0,4},{4,0},{1,5},{5,1},{2,6},{6,2},{3,7},{7,3},{8,12},{12,8},{9,1... | collective-permute-start | bytes 49160 | tf_op jit(solution)/shard_map/ppermute | solution.py:39
  26.8 4.0 %collective-permute-start.6 = (f32[2,4,1,8,128]{4,3,2,1,0:T(8,128)S(1)}, f32[2,4,1,8,128]{4,3,2,1,0:T(8,128)S(1)}, u32[]{:S(2)}, u32[]{:S(2)}) collective-permute-start(f32[2,4,1,8,128]{4,3,2,1,0:T(8,128)S(1)} %get-tuple-element.36), channel_id=1, source_target_pairs={{0,1},{1,2},{2,3},{3,0},{4,5},{5,6},{6,7},{7,4},{8,9},{9,10},{10,1... | collective-permute-start | bytes 98312 | tf_op jit(solution)/shard_map/ppermute | solution.py:43
  26.9 4.0 %collective-permute-start.7 = (f32[2,4,1,8,128]{4,3,2,1,0:T(8,128)S(1)}, f32[2,4,1,8,128]{4,3,2,1,0:T(8,128)S(1)}, u32[]{:S(2)}, u32[]{:S(2)}) collective-permute-start(f32[2,4,1,8,128]{4,3,2,1,0:T(8,128)S(1)} %get-tuple-element.37), channel_id=1, source_target_pairs={{0,3},{1,0},{2,1},{3,2},{4,7},{5,4},{6,5},{7,6},{8,11},{9,8},{10,9... | collective-permute-start | bytes 98312 | tf_op jit(solution)/shard_map/ppermute | solution.py:44
  30.9 7.1 %collective-permute-start.8 = (f32[1,4,4,8,128]{4,3,2,1,0:T(8,128)S(1)}, f32[1,4,4,8,128]{4,3,2,1,0:T(8,128)S(1)}, u32[]{:S(2)}, u32[]{:S(2)}) collective-permute-start(f32[1,4,4,8,128]{4,3,2,1,0:T(8,128)S(1)} %get-tuple-element.32), channel_id=1, source_target_pairs={{0,8},{8,16},{16,24},{24,0},{1,9},{9,17},{17,25},{25,1},{2,10},{10... | collective-permute-start | bytes 196616 | tf_op jit(solution)/shard_map/ppermute | solution.py:43
  36.6 4.3 %collective-permute-start.9 = (f32[1,4,4,8,128]{4,3,2,1,0:T(8,128)S(1)}, f32[1,4,4,8,128]{4,3,2,1,0:T(8,128)S(1)}, u32[]{:S(2)}, u32[]{:S(2)}) collective-permute-start(f32[1,4,4,8,128]{4,3,2,1,0:T(8,128)S(1)} %get-tuple-element.33), channel_id=1, source_target_pairs={{0,24},{8,0},{16,8},{24,16},{1,25},{9,1},{17,9},{25,17},{2,26},{10... | collective-permute-start | bytes 196616 | tf_op jit(solution)/shard_map/ppermute | solution.py:44
  52.3 4.5 %collective-permute-start.10 = (f32[8,128]{1,0:T(8,128)S(1)}, f32[8,128]{1,0:T(8,128)S(1)}, u32[]{:S(2)}, u32[]{:S(2)}) collective-permute-start(f32[8,128]{1,0:T(8,128)S(1)} %get-tuple-element.26), channel_id=1, source_target_pairs={{0,8},{8,16},{16,24},{24,0},{1,9},{9,17},{17,25},{25,1},{2,10},{10... | collective-permute-start | bytes 12296 | tf_op jit(solution)/shard_map/ppermute | solution.py:370
  54.4 3.6 %collective-permute-start.11 = (f32[8,128]{1,0:T(8,128)S(1)}, f32[8,128]{1,0:T(8,128)S(1)}, u32[]{:S(2)}, u32[]{:S(2)}) collective-permute-start(f32[8,128]{1,0:T(8,128)S(1)} %get-tuple-element.27), channel_id=1, source_target_pairs={{0,24},{8,0},{16,8},{24,16},{1,25},{9,1},{17,9},{25,17},{2,26},{10... | collective-permute-start | bytes 12296 | tf_op jit(solution)/shard_map/ppermute | solution.py:371
where the time goes:
time: 58.9 us; the launch traced here: 58.6 us
  Pallas kernels  24.8 us (42%)
  waiting for transfers between devices  16.9 us (29%)
  starting transfers between devices  15.4 us (26%)
  between operations  0.76 us (1%)
  local copies, waits for them, and re-layouts  0.64 us (1%)
    pallas_call x6, Pallas kernels, call(): pl.pallas_call(functools.partial(kernel, cells), out_shape=[out if hasatt...  24.8 us
    ppermute x4, starting transfers between devices, exchange(): lax.ppermute(last, axis, [(i, (i + 1) % count) for i in range(count)])  8.3 us
    ppermute x4, waiting for transfers between devices, exchange(): lax.ppermute(last, axis, [(i, (i + 1) % count) for i in range(count)])  7.06 us
    ppermute x4, waiting for transfers between devices, exchange(): lax.ppermute(first, axis, [(i, (i - 1) % count) for i in range(count)])  5.41 us
    ppermute x4, starting transfers between devices, exchange(): lax.ppermute(first, axis, [(i, (i - 1) % count) for i in range(count)])  4 us
    ppermute x2, waiting for transfers between devices, exchange(): got = lax.ppermute(jnp.where(at == 0, last, first), axis, [(0, 1), (1, 0)])  2.34 us
    ppermute x1, starting transfers between devices, body(): lax.ppermute(upper, 'gx', [(i, (i - 1) % count) for i in range(count)])  1.52 us
    ppermute x1, starting transfers between devices, body(): lax.ppermute(lower, 'gx', [(i, (i + 1) % count) for i in range(count)])  1.44 us
  transfers between devices with their start and end apart: 12, of which 12 were waited for; matrix products, arithmetic and copies ran while one was open for 0% of the time, Pallas kernels for 3%

commit v1 on v0

--- a/solution.py
+++ b/solution.py
@@ -48,9 +48,8 @@
 
 
 def with_halo(tiles):
-    for axis, dim in (("gy", 1), ("gz", 2), ("gx", 0)):
-        tiles = exchange(tiles, axis, dim)
-    return tiles
+    part = exchange(exchange(tiles, "gy", 1), "gz", 2)
+    return part, exchange(part, "gx", 0)
 
 
 def split3(values):
@@ -108,36 +107,47 @@
     return safe * (1.0 / VISC_SCALE), STIFFNESS * (square * square * square * safe - 1.0) / square
 
 
-def count_cells(halo_ref, counts):
+def count_cells(halo_ref, counts, first):
     for x in range(halo_ref.shape[0]):
         for y in range(halo_ref.shape[1]):
             live = (halo_ref[x, y, :, 7] > 0).astype(jnp.float32)
             column = jnp.sum(live, axis=1, keepdims=True).astype(jnp.int32)
             for z in range(halo_ref.shape[2]):
-                counts[x, y, z] = column[z, 0]
-
-
-def compact(halo_ref, counts, near, blocks, cells):
+                counts[x + first, y, z] = column[z, 0]
+
+
+def neighbours(cells, inner):
+    return [
+        [
+            (x, y, z)
+            for x in range(cx, cx + 3)
+            for y in range(cy, cy + 3)
+            for z in range(cz, cz + 3)
+            if (1 <= x <= cells[0]) == inner
+        ]
+        for cx, cy, cz in all_cells(cells)
+    ]
+
+
+def compact(load, counts, near, cells, lists, starts):
     lane = lax.broadcasted_iota(jnp.int32, (FIELDS, 128), 1)
     row = lax.broadcasted_iota(jnp.int32, (FIELDS, 128), 0)
-    places = all_cells(cells)
-    at = [jnp.int32(0)] * len(places)
-    for sx in range(3):
-        for sy in range(3):
-            for sz in range(3):
-                shift = jnp.where(row == 0, sx - 1.5, jnp.where(row == 1, sy - 1.5, jnp.where(row == 2, sz - 1.5, 0.0)))
-                for c, (cx, cy, cz) in enumerate(places):
-                    block, inside = lax.shift_right_logical(at[c], 7), at[c] & 127
-                    rolled = pltpu.roll(halo_ref[cx + sx, cy + sy, cz + sz] + shift, inside, axis=1)
-                    pltpu.store(near.at[c, block], rolled, mask=lane >= inside)
-                    near[c, block + 1] = rolled
-                    at[c] = at[c] + counts[cx + sx, cy + sy, cz + sz]
-    for c in range(len(places)):
-        block, inside = lax.shift_right_logical(at[c], 7), at[c] & 127
-        zeros = jnp.zeros((FIELDS, 128), jnp.float32)
-        pltpu.store(near.at[c, block], zeros, mask=lane >= inside)
-        near[c, block + 1] = zeros
-        blocks[c] = lax.shift_right_logical(at[c] + 255, 8)
+    at, shifts = list(starts), {}
+    for step in range(max(len(entries) for entries in lists)):
+        for c, own in enumerate(all_cells(cells)):
+            if step >= len(lists[c]):
+                continue
+            place = lists[c][step]
+            shift = tuple(place[k] - own[k] - 1.5 for k in range(3))
+            if shift not in shifts:
+                sx, sy, sz = shift
+                shifts[shift] = jnp.where(row == 0, sx, jnp.where(row == 1, sy, jnp.where(row == 2, sz, 0.0)))
+            block, inside = lax.shift_right_logical(at[c], 7), at[c] & 127
+            rolled = pltpu.roll(load(place) + shifts[shift], inside, axis=1)
+            pltpu.store(near.at[c, block], rolled, mask=lane >= inside)
+            near[c, block + 1] = rolled
+            at[c] = at[c] + counts[place]
+    return at
 
 
 def own_kernel(cells, tiles_ref, own_ref, terms_ref):
@@ -211,31 +221,61 @@
         pl.when(chunks == rows // 16)(functools.partial(run, rows))
 
 
-def over_cells(halo_ref, own, terms, scratch, cells, visit):
-    counts, blocks, near, total = scratch[:4]
-    count_cells(halo_ref, counts)
-    compact(halo_ref, counts, near, blocks, cells)
-
+def sum_lists(counts, near, blocks, own, terms, slots, total, cells):
     def one(index, carry):
         cz = index % cells[2]
         cy = lax.div(index, cells[2]) % cells[1]
         cx = lax.div(index, cells[1] * cells[2])
-        pair_sums(counts, near, blocks, own, terms, (scratch[4:6], scratch[6:8]), total, (cx, cy, cz), index)
+        pair_sums(counts, near, blocks, own, terms, slots, total, (cx, cy, cz), index)
         return carry
 
     lax.fori_loop(0, cells[0] * cells[1] * cells[2], one, 0)
+
+
+def inner_kernel(cells, part_ref, own, terms, total, left, *scratch):
+    counts, blocks, near = scratch[:3]
+    count_cells(part_ref, counts, 1)
+    lists = neighbours(cells, True)
+    starts = [jnp.int32(0)] * len(lists)
+    at = compact(lambda place: part_ref[place[0] - 1, place[1], place[2]], counts, near, cells, lists, starts)
+    for c in range(len(lists)):
+        blocks[c] = lax.shift_right_logical(at[c], 8)
+    sum_lists(counts, near, blocks, own, terms, (scratch[3:5], scratch[5:7]), total, cells)
+    for c in range(len(lists)):
+        for side in range(2):
+            left[c, side] = near[c, 2 * blocks[c] + side]
+
+
+def over_cells(halo_ref, own, terms, inner, left, scratch, cells, visit):
+    counts, blocks, near, total = scratch[:4]
+    count_cells(halo_ref, counts, 0)
+    lists = neighbours(cells, False)
+    starts = []
+    for c, places in enumerate(neighbours(cells, True)):
+        starts.append(sum(counts[place] for place in places) & 255)
+        for side in range(2):
+            near[c, side] = left[c, side]
+    at = compact(lambda place: halo_ref[place], counts, near, cells, lists, starts)
+    lanes = lax.broadcasted_iota(jnp.int32, (FIELDS, 128), 1)
+    for c in range(len(lists)):
+        block, inside = lax.shift_right_logical(at[c], 7), at[c] & 127
+        zeros = jnp.zeros((FIELDS, 128), jnp.float32)
+        pltpu.store(near.at[c, block], zeros, mask=lanes >= inside)
+        near[c, block + 1] = zeros
+        blocks[c] = lax.shift_right_logical(at[c] + 255, 8)
+    sum_lists(counts, near, blocks, own, terms, (scratch[4:6], scratch[6:8]), total, cells)
     ones = jnp.ones((16, 128), jnp.bfloat16)
     lane = lax.broadcasted_iota(jnp.int32, (1, 128), 1)
     for index in range(cells[0] * cells[1] * cells[2]):
         cx, cy, cz = index // (cells[1] * cells[2]), index // cells[2] % cells[1], index % cells[2]
-        flat = total[index, 1:4].reshape(3 * 128, 128)
+        flat = (inner[index, 1:4] + total[index, 1:4]).reshape(3 * 128, 128)
         high = flat.astype(jnp.bfloat16)
         middle = (flat - high.astype(jnp.float32)).astype(jnp.bfloat16)
         summed = sum(
             lax.dot_general(ones, piece, (((1,), (1,)), ((), ())), preferred_element_type=jnp.float32)[0:1]
             for piece in (high, middle)
         )
-        across = [jnp.sum(jnp.transpose(total[index, k]), axis=0, keepdims=True) for k in (0, 4)]
+        across = [jnp.sum(jnp.transpose(inner[index, k] + total[index, k]), axis=0, keepdims=True) for k in (0, 4)]
         sums = [across[0]] + [summed[:, 128 * k : 128 * (k + 1)] for k in range(3)] + [across[1]]
         tile = halo_ref[cx + 1, cy + 1, cz + 1]
         live = lane < counts[cx + 1, cy + 1, cz + 1]
@@ -245,14 +285,15 @@
         visit(cx, cy, cz, accel, jnp.where(live, -sums[4], 0.0))
 
 
-def scratch_for(halo_shape, cells):
+def scratch_for(cells, last):
     own = cells[0] * cells[1] * cells[2]
     slot = [pltpu.VMEM((2, 128, 256), jnp.float32), pltpu.VMEM((2, FIELDS, 128), jnp.float32)]
+    total = [pltpu.VMEM((own, 5, 128, 128), jnp.float32)] if last else []
     return [
-        pltpu.SMEM(halo_shape[:3], jnp.int32),
+        pltpu.SMEM(tuple(size + 2 for size in cells), jnp.int32),
         pltpu.SMEM((own,), jnp.int32),
         pltpu.VMEM((own, 32, FIELDS, 128), jnp.float32),
-        pltpu.VMEM((own, 5, 128, 128), jnp.float32),
+        *total,
         *slot,
         *slot,
     ]
@@ -300,16 +341,18 @@
         target_ref[cx, cy, here] = jnp.where(live, target, -2)
 
 
-def half_kernel(cells, halo_ref, own_ref, terms_ref, half_ref, *scratch):
+def half_kernel(cells, halo_ref, own_ref, terms_ref, inner_ref, left_ref, half_ref, *scratch):
     def visit(cx, cy, cz, accel, rate):
         tile = halo_ref[cx + 1, cy + 1, cz + 1]
         change = jnp.concatenate([tile[3:6]] + accel + [rate, jnp.zeros_like(rate)], 0)
         half_ref[cx, cy, cz] = tile + HALF_STEP * change
 
-    over_cells(halo_ref, own_ref, terms_ref, scratch, cells, visit)
-
-
-def last_kernel(cells, halo_ref, own_ref, terms_ref, state_ref, target_ref, lower_ref, upper_ref, kept_ref, *scratch):
+    over_cells(halo_ref, own_ref, terms_ref, inner_ref, left_ref, scratch, cells, visit)
+
+
+def last_kernel(
+    cells, halo_ref, own_ref, terms_ref, inner_ref, left_ref, state_ref, target_ref, lower_ref, upper_ref, kept_ref, *scratch
+):
     slots = lax.broadcasted_iota(jnp.int32, (2 * MOVES, 128), 0)
     row = lax.broadcasted_iota(jnp.int32, (FIELDS, 128), 0)
     lists = [jnp.zeros((FIELDS, 2 * MOVES), jnp.float32)]
@@ -329,7 +372,7 @@
                 piece.astype(jnp.bfloat16), chosen, (((1,), (1,)), ((), ())), preferred_element_type=jnp.float32
             )
 
-    over_cells(halo_ref, own_ref, terms_ref, scratch, cells, visit)
+    over_cells(halo_ref, own_ref, terms_ref, inner_ref, left_ref, scratch, cells, visit)
     for side, (out_ref, moved) in enumerate(((lower_ref, -float(cells[0])), (upper_ref, float(cells[0])))):
         half = lists[0][:, MOVES * side : MOVES * (side + 1)]
         out_ref[...] = half + jnp.where(row == 0, moved, 0.0) * half[7:8]
@@ -355,13 +398,18 @@
     state, target = call(state_kernel, cells, [tiles, places], fields, staged, source=pltpu.HBM)
     own = cells[0] * cells[1] * cells[2]
     sides = [jax.ShapeDtypeStruct((own, 256, 128), jnp.bfloat16), (own, 2, 128, 128)]
-    halo = with_halo(state)
-    prepared = call(own_kernel, cells, sides, (state,), cost=PREPARE)
-    scratch = scratch_for(halo.shape, cells)
-    (half,) = call(half_kernel, cells, [tiles], (halo, *prepared), scratch)
-    halo = with_halo(half)
-    prepared = call(own_kernel, cells, sides, (half,), cost=PREPARE)
-    arguments = (halo, *prepared, state, target)
+    sums = [(own, 5, 128, 128), (own, 2, FIELDS, 128)]
+
+    def gather(values):
+        part, halo = with_halo(values)
+        prepared = call(own_kernel, cells, sides, (values,), cost=PREPARE)
+        inner = call(inner_kernel, cells, sums, (part, *prepared), scratch_for(cells, False), cost=PREPARE)
+        return (halo, *prepared, *inner)
+
+    scratch = scratch_for(cells, True)
+    arguments = gather(state)
+    (half,) = call(half_kernel, cells, [tiles], arguments, scratch)
+    arguments = (*gather(half), state, target)
     lower, upper, kept = call(last_kernel, cells, [(FIELDS, MOVES), (FIELDS, MOVES), tiles], arguments, scratch)
     shapes = [offsets.shape, velocity.shape, density.shape]
     count, at = lax.axis_size("gx"), lax.axis_index("gx")

time: 58.9 us -> 56.9 us (0.966)
  the two profiles are of different devices: /device:TPU:8 before, /device:TPU:10 now
where the time goes in v1:
time: 56.9 us; the launch traced here: 56.7 us
  Pallas kernels  27.4 us (48%)
  waiting for transfers between devices  13.9 us (24%)
  starting transfers between devices  13.7 us (24%)
  between operations  0.82 us (1%)
  local copies, waits for them, and re-layouts  0.64 us (1%)
    pallas_call x8, Pallas kernels, call(): pl.pallas_call(functools.partial(kernel, cells), out_shape=[out if hasatt...  27.4 us
    ppermute x4, starting transfers between devices, exchange(): lax.ppermute(last, axis, [(i, (i + 1) % count) for i in range(count)])  8.77 us
    ppermute x4, waiting for transfers between devices, exchange(): lax.ppermute(first, axis, [(i, (i - 1) % count) for i in range(count)])  5.4 us
    ppermute x1, waiting for transfers between devices, body(): lax.ppermute(upper, 'gx', [(i, (i - 1) % count) for i in range(count)])  3.8 us
    ppermute x1, starting transfers between devices, body(): lax.ppermute(lower, 'gx', [(i, (i + 1) % count) for i in range(count)])  3.38 us
    ppermute x2, waiting for transfers between devices, exchange(): got = lax.ppermute(jnp.where(at == 0, last, first), axis, [(0, 1), (1, 0)])  2.01 us
    ppermute x4, waiting for transfers between devices, exchange(): lax.ppermute(last, axis, [(i, (i + 1) % count) for i in range(count)])  1.97 us
  transfers between devices with their start and end apart: 12, of which 8 were waited for; matrix products, arithmetic and copies ran while one was open for 0% of the time, Pallas kernels for 24%

profile of v1, /device:TPU:10, one launch (start us, length us, event | category | flops | bytes accessed | tf_op | source)
XLA Modules:
  0.0 56.7 jit_solution(15507692055156351283)
XLA Ops:
  0.6 0.9 %shard_map.102 = (f32[2,2,2,8,128]{4,3,2,1,0:T(8,128)S(1)}, s32[2,2,2,128]{3,2,1,0:T(2,128)S(1)}) custom-call(f32[3,2,2,2,128]{4,3,2,1,0:T(2,128)} %refs_0_.1, f32[3,2,2,2,128]{4,3,2,1,0:T(2,128)} %refs_1_.1, f32[2,2,2,128]{3,2,1,0:T(2,128)} %refs_2_.1, f32[2,2,2,128]{3,2,1,0:T(2,128)} %refs_3_.1, s32[2,2,2,128]{3,2,1,0:T(2,128)} %refs_4_.1, ...), custom_call_target="tpu_custom_call" | custom-call | tf_op jit(solution)/shard_map/pallas_call | solution.py:307
  1.6 0.1 collective-permute-start
  1.7 1.2 %collective-permute-done = f32[2,1,2,8,128]{4,3,2,1,0:T(8,128)S(1)} collective-permute-done((f32[2,1,2,8,128]{4,3,2,1,0:T(8,128)S(1)}, f32[2,1,2,8,128]{4,3,2,1,0:T(8,128)S(1)}, u32[]{:S(2)}, u32[]{:S(2)}) %collective-permute-start) | collective-permute-done | bytes 16416 | tf_op jit(solution)/shard_map/ppermute | solution.py:39
  2.9 1.6 %collective-permute-start.1 = (f32[2,4,1,8,128]{4,3,2,1,0:T(8,128)S(1)}, f32[2,4,1,8,128]{4,3,2,1,0:T(8,128)S(1)}, u32[]{:S(2)}, u32[]{:S(2)}) collective-permute-start(f32[2,4,1,8,128]{4,3,2,1,0:T(8,128)S(1)} %get-tuple-element.46), channel_id=1, source_target_pairs={{0,1},{1,2},{2,3},{3,0},{4,5},{5,6},{6,7},{7,4},{8,9},{9,10},{10,1... | collective-permute-start | bytes 98312 | tf_op jit(solution)/shard_map/ppermute | solution.py:43
  4.5 0.7 %shard_map.103 = (bf16[8,256,128]{2,1,0:T(8,128)(2,1)S(1)}, f32[8,2,128,128]{3,2,1,0:T(8,128)S(1)}) custom-call(f32[2,2,2,8,128]{4,3,2,1,0:T(8,128)S(1)} %get-tuple-element.20.tiles_ref.state_ref), custom_call_target="tpu_custom_call" | custom-call | flops 1000000000 | bytes 1000000 | tf_op jit(solution)/shard_map/pallas_call | solution.py:307
  5.2 0.5 collective-permute-start.2
  5.7 1.1 %collective-permute-done.1 = f32[2,4,1,8,128]{4,3,2,1,0:T(8,128)S(1)} collective-permute-done((f32[2,4,1,8,128]{4,3,2,1,0:T(8,128)S(1)}, f32[2,4,1,8,128]{4,3,2,1,0:T(8,128)S(1)}, u32[]{:S(2)}, u32[]{:S(2)}) %collective-permute-start.1) | collective-permute-done | bytes 32800 | tf_op jit(solution)/shard_map/ppermute | solution.py:43
  6.8 2.3 %collective-permute-done.2 = f32[2,4,1,8,128]{4,3,2,1,0:T(8,128)S(1)} collective-permute-done((f32[2,4,1,8,128]{4,3,2,1,0:T(8,128)S(1)}, f32[2,4,1,8,128]{4,3,2,1,0:T(8,128)S(1)}, u32[]{:S(2)}, u32[]{:S(2)}) %collective-permute-start.2) | collective-permute-done | bytes 32800 | tf_op jit(solution)/shard_map/ppermute | solution.py:44
  9.2 1.5 %collective-permute-start.3 = (f32[1,4,4,8,128]{4,3,2,1,0:T(8,128)S(1)}, f32[1,4,4,8,128]{4,3,2,1,0:T(8,128)S(1)}, u32[]{:S(2)}, u32[]{:S(2)}) collective-permute-start(f32[1,4,4,8,128]{4,3,2,1,0:T(8,128)S(1)} %get-tuple-element.42), channel_id=1, source_target_pairs={{0,8},{8,16},{16,24},{24,0},{1,9},{9,17},{17,25},{25,1},{2,10},{10... | collective-permute-start | bytes 196616 | tf_op jit(solution)/shard_map/ppermute | solution.py:43
  10.8 0.5 collective-permute-start.4
  11.3 5.7 %shard_map.104 = (f32[8,5,128,128]{3,2,1,0:T(8,128)S(1)}, f32[8,2,8,128]{3,2,1,0:T(8,128)S(1)}) custom-call(f32[2,4,4,8,128]{4,3,2,1,0:T(8,128)S(1)} %pad_maximum_fusion.2.part_ref, bf16[8,256,128]{2,1,0:T(8,128)(2,1)S(1)} %get-tuple-element.21.own.own_ref, f32[8,2,128,128]{3,2,1,0:T(8,128)S(1)} %get-tuple-element.22.terms.terms_ref), custom_call_target="tpu_custom_call" | custom-call | flops 1000000000 | bytes 1000000 | tf_op jit(solution)/shard_map/pallas_call | solution.py:307
  17.0 0.0 collective-permute-done.3
  17.0 0.0 collective-permute-done.4
  17.1 6.0 %shard_map.105.tiles_ref = f32[2,2,2,8,128]{4,3,2,1,0:T(8,128)S(1)} custom-call(f32[4,4,4,8,128]{4,3,2,1,0:T(8,128)S(1)} %pad_maximum_fusion.halo_ref, bf16[8,256,128]{2,1,0:T(8,128)(2,1)S(1)} %get-tuple-element.21.own.own_ref, f32[8,2,128,128]{3,2,1,0:T(8,128)S(1)} %get-tuple-element.22.terms.terms_ref, f32[8,5,128,128]{3,2,1,0:T(8,128)S(1)} %get-tuple-element.23.inner_ref, ...), custom_call_target="tpu_custom_call" | custom-call | tf_op jit(solution)/shard_map/pallas_call | solution.py:307
  23.1 0.4 collective-permute-start.5
  23.6 0.8 %collective-permute-done.5 = f32[2,1,2,8,128]{4,3,2,1,0:T(8,128)S(1)} collective-permute-done((f32[2,1,2,8,128]{4,3,2,1,0:T(8,128)S(1)}, f32[2,1,2,8,128]{4,3,2,1,0:T(8,128)S(1)}, u32[]{:S(2)}, u32[]{:S(2)}) %collective-permute-start.5) | collective-permute-done | bytes 16416 | tf_op jit(solution)/shard_map/ppermute | solution.py:39
  24.4 3.3 %collective-permute-start.6 = (f32[2,4,1,8,128]{4,3,2,1,0:T(8,128)S(1)}, f32[2,4,1,8,128]{4,3,2,1,0:T(8,128)S(1)}, u32[]{:S(2)}, u32[]{:S(2)}) collective-permute-start(f32[2,4,1,8,128]{4,3,2,1,0:T(8,128)S(1)} %get-tuple-element.44), channel_id=1, source_target_pairs={{0,1},{1,2},{2,3},{3,0},{4,5},{5,6},{6,7},{7,4},{8,9},{9,10},{10,1... | collective-permute-start | bytes 98312 | tf_op jit(solution)/shard_map/ppermute | solution.py:43
  27.7 0.7 %shard_map.106 = (bf16[8,256,128]{2,1,0:T(8,128)(2,1)S(1)}, f32[8,2,128,128]{3,2,1,0:T(8,128)S(1)}) custom-call(f32[2,2,2,8,128]{4,3,2,1,0:T(8,128)S(1)} %shard_map.105.tiles_ref), custom_call_target="tpu_custom_call" | custom-call | flops 1000000000 | bytes 1000000 | tf_op jit(solution)/shard_map/pallas_call | solution.py:307
  28.4 0.1 collective-permute-start.7
  28.5 0.8 %collective-permute-done.6 = f32[2,4,1,8,128]{4,3,2,1,0:T(8,128)S(1)} collective-permute-done((f32[2,4,1,8,128]{4,3,2,1,0:T(8,128)S(1)}, f32[2,4,1,8,128]{4,3,2,1,0:T(8,128)S(1)}, u32[]{:S(2)}, u32[]{:S(2)}) %collective-permute-start.6) | collective-permute-done | bytes 32800 | tf_op jit(solution)/shard_map/ppermute | solution.py:43
  29.4 3.1 %collective-permute-done.7 = f32[2,4,1,8,128]{4,3,2,1,0:T(8,128)S(1)} collective-permute-done((f32[2,4,1,8,128]{4,3,2,1,0:T(8,128)S(1)}, f32[2,4,1,8,128]{4,3,2,1,0:T(8,128)S(1)}, u32[]{:S(2)}, u32[]{:S(2)}) %collective-permute-start.7) | collective-permute-done | bytes 32800 | tf_op jit(solution)/shard_map/ppermute | solution.py:44
  32.4 2.3 %collective-permute-start.8 = (f32[1,4,4,8,128]{4,3,2,1,0:T(8,128)S(1)}, f32[1,4,4,8,128]{4,3,2,1,0:T(8,128)S(1)}, u32[]{:S(2)}, u32[]{:S(2)}) collective-permute-start(f32[1,4,4,8,128]{4,3,2,1,0:T(8,128)S(1)} %get-tuple-element.40), channel_id=1, source_target_pairs={{0,8},{8,16},{16,24},{24,0},{1,9},{9,17},{17,25},{25,1},{2,10},{10... | collective-permute-start | bytes 196616 | tf_op jit(solution)/shard_map/ppermute | solution.py:43
  34.7 0.0 collective-permute-start.9
  34.7 5.8 %shard_map.107 = (f32[8,5,128,128]{3,2,1,0:T(8,128)S(1)}, f32[8,2,8,128]{3,2,1,0:T(8,128)S(1)}) custom-call(f32[2,4,4,8,128]{4,3,2,1,0:T(8,128)S(1)} %pad_maximum_fusion.3.part_ref, bf16[8,256,128]{2,1,0:T(8,128)(2,1)S(1)} %get-tuple-element.25.own.own_ref, f32[8,2,128,128]{3,2,1,0:T(8,128)S(1)} %get-tuple-element.26.terms.terms_ref), custom_call_target="tpu_custom_call" | custom-call | flops 1000000000 | bytes 1000000 | tf_op jit(solution)/shard_map/pallas_call | solution.py:307
  40.5 0.0 collective-permute-done.9
  40.6 6.9 %shard_map.108 = (f32[8,128]{1,0:T(8,128)S(1)}, f32[8,128]{1,0:T(8,128)S(1)}, f32[2,2,2,8,128]{4,3,2,1,0:T(8,128)S(1)}) custom-call(f32[4,4,4,8,128]{4,3,2,1,0:T(8,128)S(1)} %pad_maximum_fusion.1.halo_ref, bf16[8,256,128]{2,1,0:T(8,128)(2,1)S(1)} %get-tuple-element.25.own.own_ref, f32[8,2,128,128]{3,2,1,0:T(8,128)S(1)} %get-tuple-element.26.terms.terms_ref, ...), custom_call_target="tpu_custom_call" | custom-call | tf_op jit(solution)/shard_map/pallas_call | solution.py:307
  47.5 3.4 %collective-permute-start.10 = (f32[8,128]{1,0:T(8,128)S(1)}, f32[8,128]{1,0:T(8,128)S(1)}, u32[]{:S(2)}, u32[]{:S(2)}) collective-permute-start(f32[8,128]{1,0:T(8,128)S(1)} %get-tuple-element.34), channel_id=1, source_target_pairs={{0,8},{8,16},{16,24},{24,0},{1,9},{9,17},{17,25},{25,1},{2,10},{10... | collective-permute-start | bytes 12296 | tf_op jit(solution)/shard_map/ppermute | solution.py:418
  50.9 0.6 %shard_map.109 = (f32[3,2,2,2,128]{4,3,2,1,0:T(2,128)}, f32[3,2,2,2,128]{4,3,2,1,0:T(2,128)}, f32[2,2,2,128]{3,2,1,0:T(2,128)}) custom-call(f32[2,2,2,8,128]{4,3,2,1,0:T(8,128)S(1)} %get-tuple-element.30.kept_ref), custom_call_target="tpu_custom_call" | custom-call | flops 1000000000 | bytes 1000000 | tf_op jit(solution)/shard_map/pallas_call | solution.py:307
  51.5 0.0 collective-permute-start.11
  51.5 0.7 %collective-permute-done.10 = f32[8,128]{1,0:T(8,128)S(1)} collective-permute-done((f32[8,128]{1,0:T(8,128)S(1)}, f32[8,128]{1,0:T(8,128)S(1)}, u32[]{:S(2)}, u32[]{:S(2)}) %collective-permute-start.10) | collective-permute-done | bytes 4128 | tf_op jit(solution)/shard_map/ppermute | solution.py:418
  52.2 3.8 %collective-permute-done.11 = f32[8,128]{1,0:T(8,128)S(1)} collective-permute-done((f32[8,128]{1,0:T(8,128)S(1)}, f32[8,128]{1,0:T(8,128)S(1)}, u32[]{:S(2)}, u32[]{:S(2)}) %collective-permute-start.11) | collective-permute-done | bytes 4128 | tf_op jit(solution)/shard_map/ppermute | solution.py:419
  56.0 0.6 %copy.11 = f32[7,2,1,1,1,128]{5,4,3,2,1,0:T(1,128)} copy(f32[7,2,1,1,1,128]{5,0,1,4,3,2:T(8,128)S(1)} %fusion) | data formatting | bytes 14336
  (26 shorter events, 0.2 us)
Async XLA Ops:
  1.6 1.2 %collective-permute-start = (f32[2,1,2,8,128]{4,3,2,1,0:T(8,128)S(1)}, f32[2,1,2,8,128]{4,3,2,1,0:T(8,128)S(1)}, u32[]{:S(2)}, u32[]{:S(2)}) collective-permute-start(f32[2,1,2,8,128]{4,3,2,1,0:T(8,128)S(1)} %slice_select_fusion.1), channel_id=1, source_target_pairs={{0,4},{4,0},{1,5},{5,1},{2,6},{6,2},{3,7},{7,3},{8,12},{12,8},{9,1... | collective-permute-start | bytes 49160 | tf_op jit(solution)/shard_map/ppermute | solution.py:39
  2.9 4.0 %collective-permute-start.1 = (f32[2,4,1,8,128]{4,3,2,1,0:T(8,128)S(1)}, f32[2,4,1,8,128]{4,3,2,1,0:T(8,128)S(1)}, u32[]{:S(2)}, u32[]{:S(2)}) collective-permute-start(f32[2,4,1,8,128]{4,3,2,1,0:T(8,128)S(1)} %get-tuple-element.46), channel_id=1, source_target_pairs={{0,1},{1,2},{2,3},{3,0},{4,5},{5,6},{6,7},{7,4},{8,9},{9,10},{10,1... | collective-permute-start | bytes 98312 | tf_op jit(solution)/shard_map/ppermute | solution.py:43
  5.2 4.0 %collective-permute-start.2 = (f32[2,4,1,8,128]{4,3,2,1,0:T(8,128)S(1)}, f32[2,4,1,8,128]{4,3,2,1,0:T(8,128)S(1)}, u32[]{:S(2)}, u32[]{:S(2)}) collective-permute-start(f32[2,4,1,8,128]{4,3,2,1,0:T(8,128)S(1)} %get-tuple-element.47), channel_id=1, source_target_pairs={{0,3},{1,0},{2,1},{3,2},{4,7},{5,4},{6,5},{7,6},{8,11},{9,8},{10,9... | collective-permute-start | bytes 98312 | tf_op jit(solution)/shard_map/ppermute | solution.py:44
  9.2 7.8 %collective-permute-start.3 = (f32[1,4,4,8,128]{4,3,2,1,0:T(8,128)S(1)}, f32[1,4,4,8,128]{4,3,2,1,0:T(8,128)S(1)}, u32[]{:S(2)}, u32[]{:S(2)}) collective-permute-start(f32[1,4,4,8,128]{4,3,2,1,0:T(8,128)S(1)} %get-tuple-element.42), channel_id=1, source_target_pairs={{0,8},{8,16},{16,24},{24,0},{1,9},{9,17},{17,25},{25,1},{2,10},{10... | collective-permute-start | bytes 196616 | tf_op jit(solution)/shard_map/ppermute | solution.py:43
  10.8 6.3 %collective-permute-start.4 = (f32[1,4,4,8,128]{4,3,2,1,0:T(8,128)S(1)}, f32[1,4,4,8,128]{4,3,2,1,0:T(8,128)S(1)}, u32[]{:S(2)}, u32[]{:S(2)}) collective-permute-start(f32[1,4,4,8,128]{4,3,2,1,0:T(8,128)S(1)} %get-tuple-element.43), channel_id=1, source_target_pairs={{0,24},{8,0},{16,8},{24,16},{1,25},{9,1},{17,9},{25,17},{2,26},{10... | collective-permute-start | bytes 196616 | tf_op jit(solution)/shard_map/ppermute | solution.py:44
  23.1 1.3 %collective-permute-start.5 = (f32[2,1,2,8,128]{4,3,2,1,0:T(8,128)S(1)}, f32[2,1,2,8,128]{4,3,2,1,0:T(8,128)S(1)}, u32[]{:S(2)}, u32[]{:S(2)}) collective-permute-start(f32[2,1,2,8,128]{4,3,2,1,0:T(8,128)S(1)} %slice_select_fusion), channel_id=1, source_target_pairs={{0,4},{4,0},{1,5},{5,1},{2,6},{6,2},{3,7},{7,3},{8,12},{12,8},{9,1... | collective-permute-start | bytes 49160 | tf_op jit(solution)/shard_map/ppermute | solution.py:39
  24.4 4.9 %collective-permute-start.6 = (f32[2,4,1,8,128]{4,3,2,1,0:T(8,128)S(1)}, f32[2,4,1,8,128]{4,3,2,1,0:T(8,128)S(1)}, u32[]{:S(2)}, u32[]{:S(2)}) collective-permute-start(f32[2,4,1,8,128]{4,3,2,1,0:T(8,128)S(1)} %get-tuple-element.44), channel_id=1, source_target_pairs={{0,1},{1,2},{2,3},{3,0},{4,5},{5,6},{6,7},{7,4},{8,9},{9,10},{10,1... | collective-permute-start | bytes 98312 | tf_op jit(solution)/shard_map/ppermute | solution.py:43
  28.4 4.0 %collective-permute-start.7 = (f32[2,4,1,8,128]{4,3,2,1,0:T(8,128)S(1)}, f32[2,4,1,8,128]{4,3,2,1,0:T(8,128)S(1)}, u32[]{:S(2)}, u32[]{:S(2)}) collective-permute-start(f32[2,4,1,8,128]{4,3,2,1,0:T(8,128)S(1)} %get-tuple-element.45), channel_id=1, source_target_pairs={{0,3},{1,0},{2,1},{3,2},{4,7},{5,4},{6,5},{7,6},{8,11},{9,8},{10,9... | collective-permute-start | bytes 98312 | tf_op jit(solution)/shard_map/ppermute | solution.py:44
  32.4 8.1 %collective-permute-start.8 = (f32[1,4,4,8,128]{4,3,2,1,0:T(8,128)S(1)}, f32[1,4,4,8,128]{4,3,2,1,0:T(8,128)S(1)}, u32[]{:S(2)}, u32[]{:S(2)}) collective-permute-start(f32[1,4,4,8,128]{4,3,2,1,0:T(8,128)S(1)} %get-tuple-element.40), channel_id=1, source_target_pairs={{0,8},{8,16},{16,24},{24,0},{1,9},{9,17},{17,25},{25,1},{2,10},{10... | collective-permute-start | bytes 196616 | tf_op jit(solution)/shard_map/ppermute | solution.py:43
  34.7 5.8 %collective-permute-start.9 = (f32[1,4,4,8,128]{4,3,2,1,0:T(8,128)S(1)}, f32[1,4,4,8,128]{4,3,2,1,0:T(8,128)S(1)}, u32[]{:S(2)}, u32[]{:S(2)}) collective-permute-start(f32[1,4,4,8,128]{4,3,2,1,0:T(8,128)S(1)} %get-tuple-element.41), channel_id=1, source_target_pairs={{0,24},{8,0},{16,8},{24,16},{1,25},{9,1},{17,9},{25,17},{2,26},{10... | collective-permute-start | bytes 196616 | tf_op jit(solution)/shard_map/ppermute | solution.py:44
  47.5 4.7 %collective-permute-start.10 = (f32[8,128]{1,0:T(8,128)S(1)}, f32[8,128]{1,0:T(8,128)S(1)}, u32[]{:S(2)}, u32[]{:S(2)}) collective-permute-start(f32[8,128]{1,0:T(8,128)S(1)} %get-tuple-element.34), channel_id=1, source_target_pairs={{0,8},{8,16},{16,24},{24,0},{1,9},{9,17},{17,25},{25,1},{2,10},{10... | collective-permute-start | bytes 12296 | tf_op jit(solution)/shard_map/ppermute | solution.py:418
  51.5 4.5 %collective-permute-start.11 = (f32[8,128]{1,0:T(8,128)S(1)}, f32[8,128]{1,0:T(8,128)S(1)}, u32[]{:S(2)}, u32[]{:S(2)}) collective-permute-start(f32[8,128]{1,0:T(8,128)S(1)} %get-tuple-element.35), channel_id=1, source_target_pairs={{0,24},{8,0},{16,8},{24,16},{1,25},{9,1},{17,9},{25,17},{2,26},{10... | collective-permute-start | bytes 12296 | tf_op jit(solution)/shard_map/ppermute | solution.py:419
